TPU v7x, 32 devices: a whole 2x2x4 slice. The times are simulated.
32 devices in a mesh: band: 2 (over y), dom: 16 (over z, x, core).
Axes of the slice: x: 2, y: 2, z: 4, core: 2. Of those that a mesh axis runs over, the one named last changes fastest.
Arguments:
- states_in: float32 [128, 16384], P('band', 'dom'), may hold values from -6 to 6
- stiffness: float32 [343, 343], replicated, may hold values from -2 to 2, as said below
- cell_scale: float32 [96], P('dom'), may hold values from 0.5 to 2
- potential: float32 [16384], P('dom'), may hold values from 0 to 2
- inv_mass_sqrt: float32 [16384], P('dom'), may hold values from 0.25 to 1.75
- cell_nodes: int32 [96, 343], P('dom'), may hold values from 0 to 1151, as said below
- shared_nodes: int32 [2048], P('dom'), may hold values from 0 to 1023, as said below
Outputs:
- filtered: float32 [128, 16384], P('band', 'dom')
- margin: float32 [128, 128], P('band')
Inputs may be any that keep to these rules, and one draw needn't show every extreme that they name: `stiffness`: symmetric. `cell_nodes`: in the cells of a subdomain, an entry below 1024 is one of its own nodes and an entry l of 1024 or more stands for entry l - 1024 of the next subdomain's (cyclically) shared_nodes list; every value from 0 to 1151 occurs in the subdomain's cells. `shared_nodes`: the 128 entries of each subdomain are distinct.
All inputs are finite; a program needn't handle non-finite values.
Results may differ from a plain program's by a relative error of at most 0.0001.
Values sent between devices are 32-bit elements; how exact they have to be, the bound alone decides.
A program may use at most 64 MiB of HBM per device.

v0:
```python
import jax
import jax.numpy as jnp
from jax import lax
from jax.sharding import PartitionSpec as P

DEGREE = 3
center_shift = 1.0
half_width = 4.0


def passed_along(x, axis, by):
    peers = lax.axis_size(axis)
    return lax.ppermute(x, axis, [(i, (i + by) % peers) for i in range(peers)])


def per_device(
    states_in, stiffness, cell_scale, potential, inv_mass_sqrt, cell_nodes, shared_nodes
):
    owned = states_in.shape[1]
    shared_count = shared_nodes.shape[0]
    block_rows = states_in.shape[0]

    def operate(vector):
        scaled = vector * inv_mass_sqrt[None, :]
        outgoing = jnp.take(scaled, shared_nodes, axis=1)
        ghosts = passed_along(outgoing, "dom", -1)
        extended = jnp.concatenate([scaled, ghosts], axis=1)
        cellwise = jnp.take(extended, cell_nodes, axis=1)
        product = jnp.einsum(
            "bcj,kj->bck",
            cellwise,
            stiffness,
            precision=lax.Precision.HIGHEST,
            preferred_element_type=jnp.float32,
        )
        product = product * cell_scale[None, :, None]
        summed = (
            jnp.zeros((block_rows, owned + shared_count), jnp.float32)
            .at[:, cell_nodes]
            .add(product)
        )
        returned = passed_along(summed[:, owned:], "dom", 1)
        own_sums = summed[:, :owned].at[:, shared_nodes].add(returned)
        return inv_mass_sqrt[None, :] * own_sums + potential[None, :] * vector

    previous = states_in
    current = (operate(states_in) - center_shift * states_in) / half_width
    for degree_step in range(DEGREE - 1):
        following = 2.0 * (operate(current) - center_shift * current) / half_width - previous
        previous = current
        current = following
    total_nodes = owned * lax.axis_size("dom")
    contract = (((1,), (1,)), ((), ()))
    partial_gram = lax.dot_general(
        current,
        lax.all_gather(current, "band", axis=0, tiled=True),
        contract,
        precision=lax.Precision.HIGHEST,
        preferred_element_type=jnp.float32,
    )
    row_block = partial_gram
    row_block = lax.psum(row_block, "dom")
    return (current, row_block / total_nodes)


def solution(mesh):
    return jax.shard_map(
        per_device,
        mesh=mesh,
        in_specs=(P("band", "dom"), P(), P("dom"), P("dom"), P("dom"), P("dom", None), P("dom")),
        out_specs=(P("band", "dom"), P("band", None)),
        check_vma=False,
    )
```

profile of v0, /device:TPU:0, one launch (start us, length us, event | category | flops | bytes accessed | tf_op | source)
XLA Modules:
  0.0 184.3 jit_solution(14820865741324628735)
XLA Ops:
  0.6 0.0 copy-start
  0.6 0.7 compare_select_fusion.1
  1.4 0.7 compare_and_fusion.1
  2.0 0.0 copy-start.4
  2.0 1.1 copy.34
  3.2 0.9 broadcast_multiply_fusion.2
  4.1 0.6 gather_fusion
  4.7 0.1 select_bitcast_fusion.5
  4.8 5.5 %collective-permute-start = (f32[64,128]{0,1:T(8,128)S(1)}, f32[64,128]{0,1:T(8,128)S(1)}, u32[]{:S(2)}, u32[]{:S(2)}) collective-permute-start(f32[64,128]{0,1:T(8,128)S(1)} %select_bitcast_fusion.5), channel_id=1, source_target_pairs={{0,15},{1,0},{2,1},{3,2},{4,3},{5,4},{6,5},{7,6},{8,7},{9,8},{10,9... | collective-permute-start | bytes 98312 | tf_op jit(solution)/shard_map/ppermute | solution.py:13
  10.4 0.1 reshape.99
  10.4 1.8 collective-permute-done
  12.3 3.9 %gather_fusion.1 = f32[2058,64]{1,0:T(8,128)S(1)} fusion(f32[64,1152]{0,1:T(8,128)S(1)} %pad_maximum_fusion, s32[3072]{0:T(1024)S(1)} %pad_clamp_fusion), kind=kCustom, calls=%fused_computation.1.clone | custom fusion | bytes 1061928 | tf_op jit(solution)/shard_map/jit(_take)/gather | solution.py:28
  16.2 0.3 copy.35
  16.6 0.4 reshape.136
  16.9 0.0 copy-start.5
  17.0 0.1 select_bitcast_fusion.2
  17.1 0.6 copy-done.5
  17.6 1.3 fusion
  18.9 0.3 copy.52
  19.2 0.0 copy-start.2
  19.3 1.1 reshape.150
  20.3 14.7 %scatter_custom_fusion = f32[64,1152]{0,1:T(8,128)S(1)} fusion(s32[2058]{0:T(1024)S(1)} %reshape.99, f32[2058,64]{1,0:T(8,128)} %reshape.150, f32[]{:T(128)} %constant.23.clone.1), kind=kCustom, calls=%fused_computation.37 | custom fusion | flops 131712 | bytes 295424 | tf_op jit(solution)/shard_map/scatter-add | solution.py:40
  35.1 0.1 collective-permute-start.1
  35.2 6.4 %collective-permute-done.1 = f32[64,128]{0,1:T(8,128)S(1)} collective-permute-done((f32[64,128]{0,1:T(8,128)S(1)}, f32[64,128]{0,1:T(8,128)S(1)}, u32[]{:S(2)}, u32[]{:S(2)}) %collective-permute-start.1) | collective-permute-done | bytes 32800 | tf_op jit(solution)/shard_map/ppermute | solution.py:13
  41.6 1.5 scatter_custom_fusion.1
  43.0 0.5 broadcast_multiply_fusion
  43.5 0.6 gather_fusion.2
  44.1 0.1 select_bitcast_fusion.4
  44.2 0.2 collective-permute-start.2
  44.5 1.9 %collective-permute-done.2 = f32[64,128]{0,1:T(8,128)S(1)} collective-permute-done((f32[64,128]{0,1:T(8,128)S(1)}, f32[64,128]{0,1:T(8,128)S(1)}, u32[]{:S(2)}, u32[]{:S(2)}) %collective-permute-start.2) | collective-permute-done | bytes 32800 | tf_op jit(solution)/shard_map/ppermute | solution.py:13
  46.4 5.0 %gather_fusion.3 = f32[2058,64]{1,0:T(8,128)} fusion(f32[64,1152]{0,1:T(8,128)S(1)} %pad_maximum_fusion.1, s32[3072]{0:T(1024)S(1)} %pad_clamp_fusion), kind=kCustom, calls=%fused_computation.4.clone | custom fusion | bytes 1061928 | tf_op jit(solution)/shard_map/jit(_take)/gather | solution.py:28
  51.4 1.6 copy.41
  53.0 0.4 reshape.142
  53.4 0.1 select_bitcast_fusion.1
  53.5 1.3 fusion.1
  54.8 0.3 copy.53
  55.1 1.1 reshape.151
  56.2 14.7 %scatter_custom_fusion.2 = f32[64,1152]{0,1:T(8,128)S(1)} fusion(s32[2058]{0:T(1024)S(1)} %reshape.99, f32[2058,64]{1,0:T(8,128)} %reshape.151, f32[]{:T(128)} %constant.23.clone.1), kind=kCustom, calls=%fused_computation.35 | custom fusion | flops 131712 | bytes 295424 | tf_op jit(solution)/shard_map/scatter-add | solution.py:40
  70.9 0.1 collective-permute-start.3
  71.0 6.4 %collective-permute-done.3 = f32[64,128]{0,1:T(8,128)S(1)} collective-permute-done((f32[64,128]{0,1:T(8,128)S(1)}, f32[64,128]{0,1:T(8,128)S(1)}, u32[]{:S(2)}, u32[]{:S(2)}) %collective-permute-start.3) | collective-permute-done | bytes 32800 | tf_op jit(solution)/shard_map/ppermute | solution.py:13
  77.4 1.5 scatter_custom_fusion.3
  78.9 0.5 broadcast_multiply_fusion.1
  79.4 0.6 gather_fusion.4
  80.0 0.1 select_bitcast_fusion.3
  80.1 0.1 collective-permute-start.4
  80.2 1.9 %collective-permute-done.4 = f32[64,128]{0,1:T(8,128)S(1)} collective-permute-done((f32[64,128]{0,1:T(8,128)S(1)}, f32[64,128]{0,1:T(8,128)S(1)}, u32[]{:S(2)}, u32[]{:S(2)}) %collective-permute-start.4) | collective-permute-done | bytes 32800 | tf_op jit(solution)/shard_map/ppermute | solution.py:13
  82.1 5.0 %gather_fusion.5 = f32[2058,64]{1,0:T(8,128)} fusion(f32[64,1152]{0,1:T(8,128)S(1)} %pad_maximum_fusion.2, s32[3072]{0:T(1024)S(1)} %pad_clamp_fusion), kind=kCustom, calls=%fused_computation.5.clone | custom fusion | bytes 1061928 | tf_op jit(solution)/shard_map/jit(_take)/gather | solution.py:28
  87.1 1.6 copy.46
  88.7 0.4 reshape.148
  89.1 0.1 select_bitcast_fusion
  89.1 2.1 %fusion.2 = f32[6,343,64]{1,2,0:T(8,128)} fusion(f32[64,6,343]{2,1,0:T(8,128)S(1)} %select_bitcast_fusion, f32[343,343]{1,0:T(8,128)S(1)} %copy-done, f32[6]{0:T(128)S(1)} %copy-done.5), kind=kOutput, calls=%fused_computation.17 | convolution fusion | flops 542258304 | bytes 1524316 | tf_op jit(solution)/shard_map/bcj,kj->bck/dot_general | solution.py:29
  91.2 1.4 copy.54
  92.7 1.1 reshape.152
  93.7 14.7 %scatter_custom_fusion.4 = f32[64,1152]{0,1:T(8,128)S(1)} fusion(s32[2058]{0:T(1024)S(1)} %reshape.99, f32[2058,64]{1,0:T(8,128)} %reshape.152, f32[]{:T(128)} %constant.23.clone.1), kind=kCustom, calls=%fused_computation.33 | custom fusion | flops 131712 | bytes 295424 | tf_op jit(solution)/shard_map/scatter-add | solution.py:40
  108.5 0.1 collective-permute-start.5
  108.6 6.4 %collective-permute-done.5 = f32[64,128]{0,1:T(8,128)S(1)} collective-permute-done((f32[64,128]{0,1:T(8,128)S(1)}, f32[64,128]{0,1:T(8,128)S(1)}, u32[]{:S(2)}, u32[]{:S(2)}) %collective-permute-start.5) | collective-permute-done | bytes 32800 | tf_op jit(solution)/shard_map/ppermute | solution.py:13
  114.9 1.7 scatter_custom_fusion.5
  116.6 0.5 multiply_subtract_fusion
  117.1 0.2 copy.51
  117.3 0.0 copy-start.1
  117.3 7.0 %all_gather.3 = f32[128,1024]{1,0:T(8,128)S(1)} all-gather(f32[64,1024]{1,0:T(8,128)S(1)} %copy.51), channel_id=1, replica_groups=mesh['band'=2,'dom'=16] {'band'}, dimensions={0}, use_global_device_ids=true | all-gather | bytes 786432 | tf_op jit(solution)/shard_map/all_gather | solution.py:56
  124.4 1.0 fusion.21
  125.4 58.3 %psum.7 = f32[64,128]{1,0:T(8,128)S(1)} all-reduce(f32[64,128]{1,0:T(8,128)S(1)} %fusion.21), channel_id=1, replica_groups=mesh['band'=2,'dom'=16] {'dom'}, use_global_device_ids=true, to_apply=%region_6.9 | all-reduce | flops 8192 | bytes 65536 | tf_op jit(solution)/shard_map/psum | solution.py:62
  183.7 0.6 broadcast_multiply_fusion.3
  (21 shorter events, 0.3 us)
Async XLA Ops:
  0.6 16.4 %copy-start = (f32[343,343]{1,0:T(8,128)S(1)}, f32[343,343]{1,0:T(8,128)}, u32[]{:S(2)}) copy-start(f32[343,343]{1,0:T(8,128)} %param.12) | copy-start | bytes 1411792
  2.0 8.3 %copy-start.4 = (s32[6,343]{1,0:T(8,128)S(1)}, s32[6,343]{1,0:T(8,128)}, u32[]{:S(2)}) copy-start(s32[6,343]{1,0:T(8,128)} %param.16) | copy-start | bytes 24700
  4.8 7.4 %collective-permute-start = (f32[64,128]{0,1:T(8,128)S(1)}, f32[64,128]{0,1:T(8,128)S(1)}, u32[]{:S(2)}, u32[]{:S(2)}) collective-permute-start(f32[64,128]{0,1:T(8,128)S(1)} %select_bitcast_fusion.5), channel_id=1, source_target_pairs={{0,15},{1,0},{2,1},{3,2},{4,3},{5,4},{6,5},{7,6},{8,7},{9,8},{10,9... | collective-permute-start | bytes 98312 | tf_op jit(solution)/shard_map/ppermute | solution.py:13
  16.9 0.7 copy-start.5
  19.2 15.9 %copy-start.2 = (f32[1024]{0:T(1024)S(1)}, f32[1024]{0:T(1024)}, u32[]{:S(2)}) copy-start(f32[1024]{0:T(1024)} %param.15) | copy-start | bytes 12292
  20.3 22.7 %copy-start.3 = (f32[1024]{0:T(1024)S(1)}, f32[1024]{0:T(1024)}, u32[]{:S(2)}) copy-start(f32[1024]{0:T(1024)} %param.14) | copy-start | bytes 12292
  35.1 6.5 %collective-permute-start.1 = (f32[64,128]{0,1:T(8,128)S(1)}, f32[64,128]{0,1:T(8,128)S(1)}, u32[]{:S(2)}, u32[]{:S(2)}) collective-permute-start(f32[64,128]{0,1:T(8,128)S(1)} %slice.37), channel_id=1, source_target_pairs={{0,1},{1,2},{2,3},{3,4},{4,5},{5,6},{6,7},{7,8},{8,9},{9,10},{10,1... | collective-permute-start | bytes 98312 | tf_op jit(solution)/shard_map/ppermute | solution.py:13
  44.2 2.1 %collective-permute-start.2 = (f32[64,128]{0,1:T(8,128)S(1)}, f32[64,128]{0,1:T(8,128)S(1)}, u32[]{:S(2)}, u32[]{:S(2)}) collective-permute-start(f32[64,128]{0,1:T(8,128)S(1)} %select_bitcast_fusion.4), channel_id=1, source_target_pairs={{0,15},{1,0},{2,1},{3,2},{4,3},{5,4},{6,5},{7,6},{8,7},{9,8},{10,9... | collective-permute-start | bytes 98312 | tf_op jit(solution)/shard_map/ppermute | solution.py:13
  70.9 6.5 %collective-permute-start.3 = (f32[64,128]{0,1:T(8,128)S(1)}, f32[64,128]{0,1:T(8,128)S(1)}, u32[]{:S(2)}, u32[]{:S(2)}) collective-permute-start(f32[64,128]{0,1:T(8,128)S(1)} %slice.39), channel_id=1, source_target_pairs={{0,1},{1,2},{2,3},{3,4},{4,5},{5,6},{6,7},{7,8},{8,9},{9,10},{10,1... | collective-permute-start | bytes 98312 | tf_op jit(solution)/shard_map/ppermute | solution.py:13
  80.1 2.0 %collective-permute-start.4 = (f32[64,128]{0,1:T(8,128)S(1)}, f32[64,128]{0,1:T(8,128)S(1)}, u32[]{:S(2)}, u32[]{:S(2)}) collective-permute-start(f32[64,128]{0,1:T(8,128)S(1)} %select_bitcast_fusion.3), channel_id=1, source_target_pairs={{0,15},{1,0},{2,1},{3,2},{4,3},{5,4},{6,5},{7,6},{8,7},{9,8},{10,9... | collective-permute-start | bytes 98312 | tf_op jit(solution)/shard_map/ppermute | solution.py:13
  108.5 6.5 %collective-permute-start.5 = (f32[64,128]{0,1:T(8,128)S(1)}, f32[64,128]{0,1:T(8,128)S(1)}, u32[]{:S(2)}, u32[]{:S(2)}) collective-permute-start(f32[64,128]{0,1:T(8,128)S(1)} %slice.41), channel_id=1, source_target_pairs={{0,1},{1,2},{2,3},{3,4},{4,5},{5,6},{6,7},{7,8},{8,9},{9,10},{10,1... | collective-permute-start | bytes 98312 | tf_op jit(solution)/shard_map/ppermute | solution.py:13
  117.3 67.0 %copy-start.1 = (f32[64,1024]{1,0:T(8,128)}, f32[64,1024]{1,0:T(8,128)S(1)}, u32[]{:S(2)}) copy-start(f32[64,1024]{1,0:T(8,128)S(1)} %copy.51) | copy-start | bytes 786436
where the time goes:
time: 185 us; the launch traced here: 184 us
  blocking collectives  65.3 us (35%)
  other arithmetic  53.7 us (29%)
  local copies, waits for them, and re-layouts  27.8 us (15%)
  waiting for transfers between devices  24.7 us (13%)
  starting transfers between devices  5.97 us (3%)
  matrix products  5.69 us (3%)
    psum x1, blocking collectives, per_device(): row_block = lax.psum(row_block, 'dom')  58.3 us
    scatter-add x3, other arithmetic, operate(): summed = jnp.zeros((block_rows, owned + shared_count), jnp.float32).at[:,...  44.2 us
    ppermute x6, waiting for transfers between devices, passed_along(): return lax.ppermute(x, axis, [(i, (i + by) % peers) for i in range(peers)])  24.7 us
    gather x9, local copies, waits for them, and re-layouts, operate(): cellwise = jnp.take(extended, cell_nodes, axis=1)  18.5 us
    all_gather x1, blocking collectives, per_device(): lax.all_gather(current, 'band', axis=0, tiled=True)  7.04 us
    ppermute x6, starting transfers between devices, passed_along(): return lax.ppermute(x, axis, [(i, (i + by) % peers) for i in range(peers)])  5.97 us
    mul x6, local copies, waits for them, and re-layouts, operate(): product = product * cell_scale[None, :, None]  5.25 us
    dot_general x3, matrix products, operate(): jnp.einsum('bcj,kj->bck', cellwise, stiffness, precision=lax.Precision.HI...  4.7 us
  transfers between devices with their start and end apart: 6, of which 6 were waited for; matrix products, arithmetic and copies ran while one was open for 0% of the time, Pallas kernels for 0%

commit v1 on v0

--- a/solution.py
+++ b/solution.py
@@ -59,7 +59,7 @@
         preferred_element_type=jnp.float32,
     )
     row_block = partial_gram
-    row_block = lax.psum(row_block, "dom")
+    row_block = jnp.sum(lax.all_gather(row_block, "dom"), axis=0)
     return (current, row_block / total_nodes)
 
 

time: 185 us -> 147 us (0.79)
  blocking collectives: 65.3 us -> 27.2 us
    psum x1 -> x0, blocking collectives: 58.3 us -> none  [per_device(): row_block = lax.psum(row_block, 'dom')]
    all_gather x0 -> x1, blocking collectives: none -> 20.1 us  [per_device(): row_block = jnp.sum(lax.all_gather(row_block, 'dom'), axis=0)]
where the time goes in v1:
time: 147 us; the launch traced here: 146 us
  other arithmetic  53.7 us (37%)
  local copies, waits for them, and re-layouts  27.8 us (19%)
  blocking collectives  27.2 us (19%)
  waiting for transfers between devices  24.7 us (17%)
  starting transfers between devices  5.97 us (4%)
  matrix products  5.69 us (4%)
    scatter-add x3, other arithmetic, operate(): summed = jnp.zeros((block_rows, owned + shared_count), jnp.float32).at[:,...  44.2 us
    ppermute x6, waiting for transfers between devices, passed_along(): return lax.ppermute(x, axis, [(i, (i + by) % peers) for i in range(peers)])  24.7 us
    all_gather x1, blocking collectives, per_device(): row_block = jnp.sum(lax.all_gather(row_block, 'dom'), axis=0)  20.1 us
    gather x9, local copies, waits for them, and re-layouts, operate(): cellwise = jnp.take(extended, cell_nodes, axis=1)  18.5 us
    all_gather x1, blocking collectives, per_device(): lax.all_gather(current, 'band', axis=0, tiled=True)  7.04 us
    ppermute x6, starting transfers between devices, passed_along(): return lax.ppermute(x, axis, [(i, (i + by) % peers) for i in range(peers)])  5.97 us
    mul x6, local copies, waits for them, and re-layouts, operate(): product = product * cell_scale[None, :, None]  5.25 us
    dot_general x3, matrix products, operate(): jnp.einsum('bcj,kj->bck', cellwise, stiffness, precision=lax.Precision.HI...  4.7 us
  transfers between devices with their start and end apart: 6, of which 6 were waited for; matrix products, arithmetic and copies ran while one was open for 0% of the time, Pallas kernels for 0%

profile of v1, /device:TPU:0, one launch (start us, length us, event | category | flops | bytes accessed | tf_op | source)
XLA Modules:
  0.0 146.2 jit_solution(5885865176094524976)
XLA Ops:
  0.6 0.0 copy-start
  0.6 0.7 compare_select_fusion.1
  1.4 0.7 compare_and_fusion.1
  2.0 0.0 copy-start.4
  2.0 1.1 copy.34
  3.2 0.9 broadcast_multiply_fusion.2
  4.1 0.6 gather_fusion
  4.7 0.1 select_bitcast_fusion.5
  4.8 5.5 %collective-permute-start = (f32[64,128]{0,1:T(8,128)S(1)}, f32[64,128]{0,1:T(8,128)S(1)}, u32[]{:S(2)}, u32[]{:S(2)}) collective-permute-start(f32[64,128]{0,1:T(8,128)S(1)} %select_bitcast_fusion.5), channel_id=1, source_target_pairs={{0,15},{1,0},{2,1},{3,2},{4,3},{5,4},{6,5},{7,6},{8,7},{9,8},{10,9... | collective-permute-start | bytes 98312 | tf_op jit(solution)/shard_map/ppermute | solution.py:13
  10.4 0.1 reshape.99
  10.4 1.8 %collective-permute-done = f32[64,128]{0,1:T(8,128)S(1)} collective-permute-done((f32[64,128]{0,1:T(8,128)S(1)}, f32[64,128]{0,1:T(8,128)S(1)}, u32[]{:S(2)}, u32[]{:S(2)}) %collective-permute-start) | collective-permute-done | bytes 32800 | tf_op jit(solution)/shard_map/ppermute | solution.py:13
  12.3 3.9 %gather_fusion.1 = f32[2058,64]{1,0:T(8,128)S(1)} fusion(f32[64,1152]{0,1:T(8,128)S(1)} %pad_maximum_fusion, s32[3072]{0:T(1024)S(1)} %pad_clamp_fusion), kind=kCustom, calls=%fused_computation.1.clone | custom fusion | bytes 1061928 | tf_op jit(solution)/shard_map/jit(_take)/gather | solution.py:28
  16.2 0.3 copy.35
  16.6 0.4 reshape.137
  16.9 0.0 copy-start.5
  17.0 0.1 select_bitcast_fusion.2
  17.1 0.6 copy-done.5
  17.6 1.3 fusion
  18.9 0.3 copy.52
  19.2 0.0 copy-start.2
  19.3 1.1 reshape.151
  20.3 14.7 %scatter_custom_fusion = f32[64,1152]{0,1:T(8,128)S(1)} fusion(s32[2058]{0:T(1024)S(1)} %reshape.99, f32[2058,64]{1,0:T(8,128)} %reshape.151, f32[]{:T(128)} %constant.23.clone.1), kind=kCustom, calls=%fused_computation.37 | custom fusion | flops 131712 | bytes 295424 | tf_op jit(solution)/shard_map/scatter-add | solution.py:40
  35.1 0.1 collective-permute-start.1
  35.2 6.4 %collective-permute-done.1 = f32[64,128]{0,1:T(8,128)S(1)} collective-permute-done((f32[64,128]{0,1:T(8,128)S(1)}, f32[64,128]{0,1:T(8,128)S(1)}, u32[]{:S(2)}, u32[]{:S(2)}) %collective-permute-start.1) | collective-permute-done | bytes 32800 | tf_op jit(solution)/shard_map/ppermute | solution.py:13
  41.6 1.5 scatter_custom_fusion.1
  43.0 0.5 broadcast_multiply_fusion
  43.5 0.6 gather_fusion.2
  44.1 0.1 select_bitcast_fusion.4
  44.2 0.2 collective-permute-start.2
  44.5 1.9 %collective-permute-done.2 = f32[64,128]{0,1:T(8,128)S(1)} collective-permute-done((f32[64,128]{0,1:T(8,128)S(1)}, f32[64,128]{0,1:T(8,128)S(1)}, u32[]{:S(2)}, u32[]{:S(2)}) %collective-permute-start.2) | collective-permute-done | bytes 32800 | tf_op jit(solution)/shard_map/ppermute | solution.py:13
  46.4 5.0 %gather_fusion.3 = f32[2058,64]{1,0:T(8,128)} fusion(f32[64,1152]{0,1:T(8,128)S(1)} %pad_maximum_fusion.1, s32[3072]{0:T(1024)S(1)} %pad_clamp_fusion), kind=kCustom, calls=%fused_computation.4.clone | custom fusion | bytes 1061928 | tf_op jit(solution)/shard_map/jit(_take)/gather | solution.py:28
  51.4 1.6 %copy.41 = f32[2058,64]{0,1:T(8,128)S(1)} copy(f32[2058,64]{1,0:T(8,128)} %gather_fusion.3) | data formatting | bytes 1053696 | tf_op jit(solution)/shard_map/jit(_take)/gather | solution.py:28
  53.0 0.4 reshape.143
  53.4 0.1 select_bitcast_fusion.1
  53.5 1.3 fusion.1
  54.8 0.3 copy.53
  55.1 1.1 reshape.152
  56.2 14.7 %scatter_custom_fusion.2 = f32[64,1152]{0,1:T(8,128)S(1)} fusion(s32[2058]{0:T(1024)S(1)} %reshape.99, f32[2058,64]{1,0:T(8,128)} %reshape.152, f32[]{:T(128)} %constant.23.clone.1), kind=kCustom, calls=%fused_computation.35 | custom fusion | flops 131712 | bytes 295424 | tf_op jit(solution)/shard_map/scatter-add | solution.py:40
  70.9 0.1 collective-permute-start.3
  71.0 6.4 %collective-permute-done.3 = f32[64,128]{0,1:T(8,128)S(1)} collective-permute-done((f32[64,128]{0,1:T(8,128)S(1)}, f32[64,128]{0,1:T(8,128)S(1)}, u32[]{:S(2)}, u32[]{:S(2)}) %collective-permute-start.3) | collective-permute-done | bytes 32800 | tf_op jit(solution)/shard_map/ppermute | solution.py:13
  77.4 1.5 scatter_custom_fusion.3
  78.9 0.5 broadcast_multiply_fusion.1
  79.4 0.6 gather_fusion.4
  80.0 0.1 select_bitcast_fusion.3
  80.1 0.1 collective-permute-start.4
  80.2 1.9 %collective-permute-done.4 = f32[64,128]{0,1:T(8,128)S(1)} collective-permute-done((f32[64,128]{0,1:T(8,128)S(1)}, f32[64,128]{0,1:T(8,128)S(1)}, u32[]{:S(2)}, u32[]{:S(2)}) %collective-permute-start.4) | collective-permute-done | bytes 32800 | tf_op jit(solution)/shard_map/ppermute | solution.py:13
  82.1 5.0 %gather_fusion.5 = f32[2058,64]{1,0:T(8,128)} fusion(f32[64,1152]{0,1:T(8,128)S(1)} %pad_maximum_fusion.2, s32[3072]{0:T(1024)S(1)} %pad_clamp_fusion), kind=kCustom, calls=%fused_computation.5.clone | custom fusion | bytes 1061928 | tf_op jit(solution)/shard_map/jit(_take)/gather | solution.py:28
  87.1 1.6 %copy.46 = f32[2058,64]{0,1:T(8,128)S(1)} copy(f32[2058,64]{1,0:T(8,128)} %gather_fusion.5) | data formatting | bytes 1053696 | tf_op jit(solution)/shard_map/jit(_take)/gather | solution.py:28
  88.7 0.4 reshape.149
  89.1 0.1 select_bitcast_fusion
  89.1 2.1 %fusion.2 = f32[6,343,64]{1,2,0:T(8,128)} fusion(f32[64,6,343]{2,1,0:T(8,128)S(1)} %select_bitcast_fusion, f32[343,343]{1,0:T(8,128)S(1)} %copy-done, f32[6]{0:T(128)S(1)} %copy-done.5), kind=kOutput, calls=%fused_computation.17 | convolution fusion | flops 542258304 | bytes 1524316 | tf_op jit(solution)/shard_map/bcj,kj->bck/dot_general | solution.py:29
  91.2 1.4 copy.54
  92.7 1.1 reshape.153
  93.7 14.7 %scatter_custom_fusion.4 = f32[64,1152]{0,1:T(8,128)S(1)} fusion(s32[2058]{0:T(1024)S(1)} %reshape.99, f32[2058,64]{1,0:T(8,128)} %reshape.153, f32[]{:T(128)} %constant.23.clone.1), kind=kCustom, calls=%fused_computation.33 | custom fusion | flops 131712 | bytes 295424 | tf_op jit(solution)/shard_map/scatter-add | solution.py:40
  108.5 0.1 collective-permute-start.5
  108.6 6.4 %collective-permute-done.5 = f32[64,128]{0,1:T(8,128)S(1)} collective-permute-done((f32[64,128]{0,1:T(8,128)S(1)}, f32[64,128]{0,1:T(8,128)S(1)}, u32[]{:S(2)}, u32[]{:S(2)}) %collective-permute-start.5) | collective-permute-done | bytes 32800 | tf_op jit(solution)/shard_map/ppermute | solution.py:13
  114.9 1.7 %scatter_custom_fusion.5 = f32[64,1024]{0,1:T(8,128)S(1)} fusion(f32[64,1024]{0,1:T(8,128)S(1)} %slice.40, s32[128]{0:T(128)S(1)} %compare_select_fusion.1, f32[64,128]{0,1:T(8,128)S(1)} %collective-permute-done.5), kind=kCustom, calls=%fused_computation.42 | custom fusion | flops 8192 | bytes 327680 | tf_op jit(solution)/shard_map/scatter-add | solution.py:43
  116.6 0.5 multiply_subtract_fusion
  117.1 0.2 copy.51
  117.3 0.0 copy-start.1
  117.3 7.0 %all_gather.9 = f32[128,1024]{1,0:T(8,128)S(1)} all-gather(f32[64,1024]{1,0:T(8,128)S(1)} %copy.51), channel_id=1, replica_groups=mesh['band'=2,'dom'=16] {'band'}, dimensions={0}, use_global_device_ids=true | all-gather | bytes 786432 | tf_op jit(solution)/shard_map/all_gather | solution.py:56
  124.4 1.0 fusion.21
  125.4 20.1 %all-gather = f32[1024,128]{1,0:T(8,128)S(1)} all-gather(f32[64,128]{1,0:T(8,128)S(1)} %fusion.21), channel_id=2, replica_groups=mesh['band'=2,'dom'=16] {'dom'}, dimensions={0}, use_global_device_ids=true | all-gather | bytes 557056 | tf_op jit(solution)/shard_map/all_gather | solution.py:62
  145.5 0.6 broadcast_multiply_fusion.3
  (22 shorter events, 0.3 us)
Async XLA Ops:
  0.6 16.4 %copy-start = (f32[343,343]{1,0:T(8,128)S(1)}, f32[343,343]{1,0:T(8,128)}, u32[]{:S(2)}) copy-start(f32[343,343]{1,0:T(8,128)} %param.12) | copy-start | bytes 1411792
  2.0 8.3 %copy-start.4 = (s32[6,343]{1,0:T(8,128)S(1)}, s32[6,343]{1,0:T(8,128)}, u32[]{:S(2)}) copy-start(s32[6,343]{1,0:T(8,128)} %param.16) | copy-start | bytes 24700
  4.8 7.4 %collective-permute-start = (f32[64,128]{0,1:T(8,128)S(1)}, f32[64,128]{0,1:T(8,128)S(1)}, u32[]{:S(2)}, u32[]{:S(2)}) collective-permute-start(f32[64,128]{0,1:T(8,128)S(1)} %select_bitcast_fusion.5), channel_id=1, source_target_pairs={{0,15},{1,0},{2,1},{3,2},{4,3},{5,4},{6,5},{7,6},{8,7},{9,8},{10,9... | collective-permute-start | bytes 98312 | tf_op jit(solution)/shard_map/ppermute | solution.py:13
  16.9 0.7 copy-start.5
  19.2 15.9 %copy-start.2 = (f32[1024]{0:T(1024)S(1)}, f32[1024]{0:T(1024)}, u32[]{:S(2)}) copy-start(f32[1024]{0:T(1024)} %param.15) | copy-start | bytes 12292
  20.3 22.7 %copy-start.3 = (f32[1024]{0:T(1024)S(1)}, f32[1024]{0:T(1024)}, u32[]{:S(2)}) copy-start(f32[1024]{0:T(1024)} %param.14) | copy-start | bytes 12292
  35.1 6.5 %collective-permute-start.1 = (f32[64,128]{0,1:T(8,128)S(1)}, f32[64,128]{0,1:T(8,128)S(1)}, u32[]{:S(2)}, u32[]{:S(2)}) collective-permute-start(f32[64,128]{0,1:T(8,128)S(1)} %slice.37), channel_id=1, source_target_pairs={{0,1},{1,2},{2,3},{3,4},{4,5},{5,6},{6,7},{7,8},{8,9},{9,10},{10,1... | collective-permute-start | bytes 98312 | tf_op jit(solution)/shard_map/ppermute | solution.py:13
  44.2 2.1 %collective-permute-start.2 = (f32[64,128]{0,1:T(8,128)S(1)}, f32[64,128]{0,1:T(8,128)S(1)}, u32[]{:S(2)}, u32[]{:S(2)}) collective-permute-start(f32[64,128]{0,1:T(8,128)S(1)} %select_bitcast_fusion.4), channel_id=1, source_target_pairs={{0,15},{1,0},{2,1},{3,2},{4,3},{5,4},{6,5},{7,6},{8,7},{9,8},{10,9... | collective-permute-start | bytes 98312 | tf_op jit(solution)/shard_map/ppermute | solution.py:13
  70.9 6.5 %collective-permute-start.3 = (f32[64,128]{0,1:T(8,128)S(1)}, f32[64,128]{0,1:T(8,128)S(1)}, u32[]{:S(2)}, u32[]{:S(2)}) collective-permute-start(f32[64,128]{0,1:T(8,128)S(1)} %slice.39), channel_id=1, source_target_pairs={{0,1},{1,2},{2,3},{3,4},{4,5},{5,6},{6,7},{7,8},{8,9},{9,10},{10,1... | collective-permute-start | bytes 98312 | tf_op jit(solution)/shard_map/ppermute | solution.py:13
  80.1 2.0 %collective-permute-start.4 = (f32[64,128]{0,1:T(8,128)S(1)}, f32[64,128]{0,1:T(8,128)S(1)}, u32[]{:S(2)}, u32[]{:S(2)}) collective-permute-start(f32[64,128]{0,1:T(8,128)S(1)} %select_bitcast_fusion.3), channel_id=1, source_target_pairs={{0,15},{1,0},{2,1},{3,2},{4,3},{5,4},{6,5},{7,6},{8,7},{9,8},{10,9... | collective-permute-start | bytes 98312 | tf_op jit(solution)/shard_map/ppermute | solution.py:13
  108.5 6.5 %collective-permute-start.5 = (f32[64,128]{0,1:T(8,128)S(1)}, f32[64,128]{0,1:T(8,128)S(1)}, u32[]{:S(2)}, u32[]{:S(2)}) collective-permute-start(f32[64,128]{0,1:T(8,128)S(1)} %slice.41), channel_id=1, source_target_pairs={{0,1},{1,2},{2,3},{3,4},{4,5},{5,6},{6,7},{7,8},{8,9},{9,10},{10,1... | collective-permute-start | bytes 98312 | tf_op jit(solution)/shard_map/ppermute | solution.py:13
  117.3 28.2 %copy-start.1 = (f32[64,1024]{1,0:T(8,128)}, f32[64,1024]{1,0:T(8,128)S(1)}, u32[]{:S(2)}) copy-start(f32[64,1024]{1,0:T(8,128)S(1)} %copy.51) | copy-start | bytes 786436
